TPU v7x, 32 devices: a whole 2x2x4 slice. The times are simulated.
32 devices in a mesh: spatial: 8 (over z, x), filter: 4 (over y, core).
Axes of the slice: x: 2, y: 2, z: 4, core: 2. Of those that a mesh axis runs over, the one named last changes fastest.
Arguments:
- volume_in: bfloat16 [128, 32, 8192], P('filter', 'spatial'), may hold values from -6 to 6
- filters_a: bfloat16 [27, 256, 128], P(None, 'filter'), may hold values from -0.109375 to 0.109375
- bias_a: bfloat16 [256], P('filter'), may hold values from -0.5 to 0.5
- filters_b: bfloat16 [27, 256, 256], P(None, 'filter'), may hold values from -0.078125 to 0.078125
- bias_b: bfloat16 [256], P('filter'), may hold values from -0.5 to 0.5
Outputs:
- volume_out: bfloat16 [256, 8, 512], P('filter', 'spatial')
All inputs are finite; a program needn't handle non-finite values.
Results may differ from a plain program's by a relative error of at most 0.0048.
Values may be sent and summed in bfloat16 or wider, within the bound.
A program may use at most 128 MiB of HBM per device.

v0:
```python
import jax
import jax.numpy as jnp
from jax import lax
from jax.sharding import PartitionSpec as P

ROWS = 64
COLS = 128


def shifted(block, axis, distance):
    devices = range(lax.axis_size(axis))
    route = [(i - distance, i) for i in devices if i - distance in devices]
    return lax.ppermute(block, axis, route)


def local_conv(block, weight, pad_rows, row_count, col_count):
    channels = block.shape[0]
    slices = block.shape[1]
    volume = block.reshape(1, channels, slices, row_count, col_count)
    kernel = weight.reshape(3, 3, 3, weight.shape[1], weight.shape[2])
    return lax.conv_general_dilated(
        volume,
        kernel,
        (2, 2, 2),
        ((0, 0), (pad_rows, pad_rows), (1, 1)),
        dimension_numbers=("NCDHW", "DHWOI", "NCDHW"),
        preferred_element_type=jnp.float32,
    )[0]


def activate(summed, bias_vec):
    summed = summed + bias_vec.astype(jnp.float32)[:, None, None, None]
    return jnp.where(summed > 0, summed, 0.2 * summed).astype(jnp.bfloat16)


def per_device(volume_in, filters_a, bias_a, filters_b, bias_b):
    slices = volume_in.shape[1]
    outputs = filters_a.shape[1]
    beneath = shifted(volume_in[:, -1:], "spatial", 1)
    extended = jnp.concatenate([beneath, volume_in], 1)
    zeros_first = jnp.zeros((outputs, slices // 2, ROWS // 2, COLS // 2), jnp.float32)
    weight_part = filters_a
    summed = zeros_first + local_conv(
        lax.all_gather(extended, "filter", axis=0, tiled=True), weight_part, 1, ROWS, COLS
    )
    hidden = activate(summed, bias_a).reshape(outputs, slices // 2, ROWS // 2 * (COLS // 2))
    beneath_two = shifted(hidden[:, -1:], "spatial", 1)
    extended_two = jnp.concatenate([beneath_two, hidden], 1)
    zeros_second = jnp.zeros((filters_b.shape[1], slices // 4, ROWS // 4, COLS // 4), jnp.float32)
    weight_part = filters_b
    summed_two = zeros_second + local_conv(
        lax.all_gather(extended_two, "filter", axis=0, tiled=True),
        weight_part,
        1,
        ROWS // 2,
        COLS // 2,
    )
    return activate(summed_two, bias_b).reshape(
        filters_b.shape[1], slices // 4, ROWS // 4 * (COLS // 4)
    )


def solution(mesh):
    in_specs = (
        P("filter", "spatial", None),
        P(None, "filter", None),
        P("filter"),
        P(None, "filter", None),
        P("filter"),
    )
    out_specs = P("filter", "spatial", None)
    return jax.shard_map(
        per_device, mesh=mesh, in_specs=in_specs, out_specs=out_specs, check_vma=False
    )
```

profile of v0, /device:TPU:0, one launch (start us, length us, event | category | flops | bytes accessed | tf_op | source)
XLA Modules:
  0.0 223.8 jit_solution(5031182525449573084)
XLA Ops:
  6.5 0.0 copy-start
  6.5 0.0 all-gather.3.cloned.1.call-start
  6.5 2.8 %copy.46 = bf16[32,4,8192]{2,0,1:T(8,128)(2,1)S(1)} copy(bf16[32,4,8192]{2,1,0:T(4,128)(2,1)} %param.5) | data formatting | bytes 4194304 | tf_op args[0]
  9.4 0.0 copy-start.2
  9.4 4.9 %collective-permute-start = (bf16[32,1,8192]{2,0,1:T(8,128)(2,1)S(1)}, bf16[32,1,8192]{2,0,1:T(8,128)(2,1)S(1)}, u32[]{:S(2)}, u32[]{:S(2)}) collective-permute-start(bf16[32,1,8192]{2,0,1:T(8,128)(2,1)S(1)} %slice.12), channel_id=1, source_target_pairs={{0,4},{4,8},{8,12},{12,16},{16,20},{20,24},{24,28},{1,5},{5,9},{9,... | collective-permute-start | bytes 1572872 | tf_op jit(solution)/shard_map/ppermute | solution.py:13
  14.3 11.1 %collective-permute-done = bf16[32,1,8192]{2,0,1:T(8,128)(2,1)S(1)} collective-permute-done((bf16[32,1,8192]{2,0,1:T(8,128)(2,1)S(1)}, bf16[32,1,8192]{2,0,1:T(8,128)(2,1)S(1)}, u32[]{:S(2)}, u32[]{:S(2)}) %collective-permute-start) | collective-permute-done | bytes 524320 | tf_op jit(solution)/shard_map/ppermute | solution.py:13
  25.4 1.8 pad_maximum_fusion
  27.2 0.0 all-gather.3.cloned.1.call-update
  27.2 0.0 all-gather.5.cloned.1.call-start
  27.3 0.0 copy-done.2
  27.3 72.5 %all-gather.3.cloned.1.call-done = bf16[128,5,8192]{2,0,1:T(8,128)(2,1)} async-done(((bf16[32,5,8192]{2,0,1:T(8,128)(2,1)}), bf16[128,5,8192]{2,0,1:T(8,128)(2,1)}) %all-gather.3.cloned.1.call-update) | async-done | bytes 10485776 | tf_op jit(solution)/shard_map/all_gather | solution.py:44
  99.8 14.2 %copy.48 = bf16[128,5,8192]{0,2,1:T(8,128)(2,1)} copy(bf16[128,5,8192]{2,0,1:T(8,128)(2,1)} %all-gather.3.cloned.1.call-done) | data formatting | bytes 20971520 | tf_op jit(solution)/shard_map/all_gather | solution.py:44
  114.0 14.7 %copy.61 = bf16[128,5,64,1,128]{0,2,4,1,3:T(8,128)(2,1)} copy(bf16[128,5,64,1,128]{0,4,2,1,3:T(8,128)(2,1)} %bitcast.31) | data formatting | bytes 20971520
  128.8 6.4 %pad.clone = bf16[128,5,64,1,144]{0,2,4,1,3:T(8,128)(2,1)S(1)} pad(bf16[128,5,64,1,128]{0,2,4,1,3:T(8,128)(2,1)} %copy.61, bf16[]{:T(256)} %constant.1), padding=0_0x0_0x0_0x0_0x1_15 | pad | bytes 22282242 | tf_op jit(solution)/shard_map/reshape | solution.py:19
  135.2 0.0 copy-start.1
  135.2 0.0 copy-start.4
  135.2 8.6 %copy.51 = bf16[128,5,64,1,8,18]{0,4,5,2,1,3:T(8,128)(2,1)S(1)} copy(bf16[128,5,64,1,8,18]{0,2,5,4,1,3:T(8,128)(2,1)S(1)} %bitcast.30) | data formatting | bytes 23592960 | tf_op jit(solution)/shard_map/conv_general_dilated | solution.py:21
  143.9 0.3 slice.13
  144.2 0.0 copy-done.1
  144.2 0.0 copy-done.4
  144.2 10.2 %fusion.12 = f32[2,32,8,9,64]{4,2,3,1,0:T(8,128)} fusion(bf16[3,3,3,64,128]{4,3,2,1,0:T(8,128)(2,1)S(1)} %bitcast.37, bf16[128,5,64,1,7,2]{0,4,5,2,1,3:T(8,128)(2,1)S(1)} %slice.13, bf16[128,5,64,1,8,18]{0,4,5,2,1,3:T(8,128)(2,1)S(1)} %copy.51, pred[8,9]{0,1:T(8,128)(4,1)S(1)} %copy-done.4), kind=kOutput, calls=%fused_computation.15 | convolution fusion | flops 2056814592 | bytes 14565448 | tf_op jit(solution)/shard_map/conv_general_dilated | solution.py:21
  154.5 2.1 copy.52
  156.6 0.2 slice_bitcast_fusion
  156.8 3.1 %copy.53 = f32[1,64,2,32,64]{4,3,1,2,0:T(8,128)} copy(f32[1,64,2,32,64]{1,3,4,2,0:T(8,128)S(1)} %slice_bitcast_fusion) | data formatting | bytes 2097152 | tf_op jit(solution)/shard_map/conv_general_dilated | solution.py:21
  159.8 0.0 copy-start.3
  159.8 2.1 squeeze.6
  161.9 0.2 fusion.18
  162.2 3.4 %collective-permute-start.1 = (bf16[64,1,2048]{2,0,1:T(8,128)(2,1)S(1)}, bf16[64,1,2048]{2,0,1:T(8,128)(2,1)S(1)}, u32[]{:S(2)}, u32[]{:S(2)}) collective-permute-start(bf16[64,1,2048]{2,0,1:T(8,128)(2,1)S(1)} %slice.15), channel_id=1, source_target_pairs={{0,4},{4,8},{8,12},{12,16},{16,20},{20,24},{24,28},{1,5},{5,9},{9,... | collective-permute-start | bytes 786440 | tf_op jit(solution)/shard_map/ppermute | solution.py:13
  165.6 6.0 %collective-permute-done.1 = bf16[64,1,2048]{2,0,1:T(8,128)(2,1)S(1)} collective-permute-done((bf16[64,1,2048]{2,0,1:T(8,128)(2,1)S(1)}, bf16[64,1,2048]{2,0,1:T(8,128)(2,1)S(1)}, u32[]{:S(2)}, u32[]{:S(2)}) %collective-permute-start.1) | collective-permute-done | bytes 262176 | tf_op jit(solution)/shard_map/ppermute | solution.py:13
  171.5 1.0 pad_maximum_fusion.1
  172.5 0.0 all-gather.5.cloned.1.call-update
  172.5 0.0 copy-done.3
  172.6 29.7 %all-gather.5.cloned.1.call-done = bf16[256,3,2048]{2,0,1:T(8,128)(2,1)} async-done(((bf16[64,3,2048]{2,0,1:T(8,128)(2,1)}), bf16[256,3,2048]{2,0,1:T(8,128)(2,1)}) %all-gather.5.cloned.1.call-update) | async-done | bytes 3145744 | tf_op jit(solution)/shard_map/all_gather | solution.py:52
  202.2 4.6 %copy.54 = bf16[256,3,2048]{0,2,1:T(8,128)(2,1)} copy(bf16[256,3,2048]{2,0,1:T(8,128)(2,1)} %all-gather.5.cloned.1.call-done) | data formatting | bytes 6291456 | tf_op jit(solution)/shard_map/all_gather | solution.py:52
  206.9 3.7 %copy.62 = bf16[256,3,32,1,64]{0,2,4,1,3:T(8,128)(2,1)S(1)} copy(bf16[256,3,32,1,64]{0,4,2,1,3:T(8,128)(2,1)} %bitcast.33) | data formatting | bytes 6291456
  210.6 0.4 pad.2.clone
  211.0 0.0 copy-start.5
  211.0 2.3 %copy.57 = bf16[256,3,32,1,8,10]{0,4,5,2,1,3:T(8,128)(2,1)S(1)} copy(bf16[256,3,32,1,8,10]{0,2,5,4,1,3:T(8,128)(2,1)S(1)} %bitcast.32) | data formatting | bytes 7864320 | tf_op jit(solution)/shard_map/conv_general_dilated | solution.py:21
  213.3 0.2 slice.16
  213.5 0.0 copy-done
  213.5 0.0 copy-done.5
  213.5 2.5 %fusion.15 = f32[1,16,8,5,64]{4,2,3,1,0:T(8,128)S(1)} fusion(bf16[3,3,3,64,256]{4,3,2,1,0:T(8,128)(2,1)S(1)} %bitcast.29, bf16[256,3,32,1,7,2]{0,4,5,2,1,3:T(8,128)(2,1)S(1)} %slice.16, bf16[256,3,32,1,8,10]{0,4,5,2,1,3:T(8,128)(2,1)S(1)} %copy.57, pred[8,5]{0,1:T(8,128)(4,1)S(1)} %copy-done.5), kind=kOutput, calls=%fused_computation.16 | convolution fusion | flops 568631296 | bytes 5668904 | tf_op jit(solution)/shard_map/conv_general_dilated | solution.py:21
  216.0 0.1 copy.58
  216.1 0.1 copy.59
  216.1 0.1 copy.60
  216.3 0.7 fusion.19
  (5 shorter events, 0.1 us)
Async XLA Ops:
  6.5 206.9 %copy-start = (bf16[27,64,256]{2,1,0:T(8,128)(2,1)S(1)}, bf16[27,64,256]{2,1,0:T(8,128)(2,1)}, u32[]{:S(2)}) copy-start(bf16[27,64,256]{2,1,0:T(8,128)(2,1)} %param.8) | copy-start | bytes 2654212
  6.5 93.3 %all-gather.3.cloned.1.call-start = ((), (), s32[]{:S(2)}) async-start(), calls=%async_computation | async-start | bytes 13107200 | tf_op jit(solution)/shard_map/all_gather | solution.py:44
  9.4 17.9 %copy-start.2 = (bf16[64]{0:T(256)(128)(2,1)S(1)}, bf16[64]{0:T(256)(128)(2,1)}, u32[]{:S(2)}) copy-start(bf16[64]{0:T(256)(128)(2,1)} %param.7) | copy-start | bytes 388
  9.4 16.0 %collective-permute-start = (bf16[32,1,8192]{2,0,1:T(8,128)(2,1)S(1)}, bf16[32,1,8192]{2,0,1:T(8,128)(2,1)S(1)}, u32[]{:S(2)}, u32[]{:S(2)}) collective-permute-start(bf16[32,1,8192]{2,0,1:T(8,128)(2,1)S(1)} %slice.12), channel_id=1, source_target_pairs={{0,4},{4,8},{8,12},{12,16},{16,20},{20,24},{24,28},{1,5},{5,9},{9,... | collective-permute-start | bytes 1572872 | tf_op jit(solution)/shard_map/ppermute | solution.py:13
  27.2 175.0 %all-gather.5.cloned.1.call-start = ((), (), s32[]{:S(2)}) async-start(), calls=%async_computation.1 | async-start | bytes 3932160 | tf_op jit(solution)/shard_map/all_gather | solution.py:52
  135.2 9.0 %copy-start.1 = (bf16[27,64,128]{2,1,0:T(8,128)(2,1)S(1)}, bf16[27,64,128]{2,1,0:T(8,128)(2,1)}, u32[]{:S(2)}) copy-start(bf16[27,64,128]{2,1,0:T(8,128)(2,1)} %param.6) | copy-start | bytes 1327108
  135.2 9.0 %copy-start.4 = (pred[8,9]{0,1:T(8,128)(4,1)S(1)}, pred[8,9]{0,1:T(8,128)(4,1)}, u32[]{:S(2)}) copy-start(pred[8,9]{0,1:T(8,128)(4,1)} %constant.16) | copy-start | bytes 220
  159.8 12.7 %copy-start.3 = (bf16[64]{0:T(256)(128)(2,1)S(1)}, bf16[64]{0:T(256)(128)(2,1)}, u32[]{:S(2)}) copy-start(bf16[64]{0:T(256)(128)(2,1)} %param.9) | copy-start | bytes 388
  162.2 9.4 %collective-permute-start.1 = (bf16[64,1,2048]{2,0,1:T(8,128)(2,1)S(1)}, bf16[64,1,2048]{2,0,1:T(8,128)(2,1)S(1)}, u32[]{:S(2)}, u32[]{:S(2)}) collective-permute-start(bf16[64,1,2048]{2,0,1:T(8,128)(2,1)S(1)} %slice.15), channel_id=1, source_target_pairs={{0,4},{4,8},{8,12},{12,16},{16,20},{20,24},{24,28},{1,5},{5,9},{9,... | collective-permute-start | bytes 786440 | tf_op jit(solution)/shard_map/ppermute | solution.py:13
  211.0 2.5 %copy-start.5 = (pred[8,5]{0,1:T(8,128)(4,1)S(1)}, pred[8,5]{0,1:T(8,128)(4,1)}, u32[]{:S(2)}) copy-start(pred[8,5]{0,1:T(8,128)(4,1)} %constant.15) | copy-start | bytes 124
Sparse Core Ops, SparseCore 0:
  27.4 72.4 all-gather.2
  172.7 29.5 all-gather.4
where the time goes:
time: 225 us; the launch traced here: 224 us
  waiting for transfers between devices  119 us (53%)
  local copies, waits for them, and re-layouts  66.2 us (29%)
  between operations  13.6 us (6%)
  matrix products  12.7 us (6%)
  starting transfers between devices  8.31 us (4%)
  other arithmetic  3.7 us (2%)
    all_gather x1, waiting for transfers between devices, per_device(): lax.all_gather(extended, 'filter', axis=0, tiled=True)  72.5 us
    all_gather x1, waiting for transfers between devices, per_device(): lax.all_gather(extended_two, 'filter', axis=0, tiled=True)  29.7 us
    unnamed x15, local copies, waits for them, and re-layouts  21.3 us
    ppermute x2, waiting for transfers between devices, shifted(): return lax.ppermute(block, axis, route)  17.1 us
    conv_general_dilated x10, local copies, waits for them, and re-layouts, local_conv(): lax.conv_general_dilated(volume, kernel, (2, 2, 2), ((0, 0), (pad_rows, p...  17 us
    all_gather x1, local copies, waits for them, and re-layouts, per_device(): lax.all_gather(extended, 'filter', axis=0, tiled=True)  14.2 us
    conv_general_dilated x2, matrix products, local_conv(): lax.conv_general_dilated(volume, kernel, (2, 2, 2), ((0, 0), (pad_rows, p...  12.7 us
    ppermute x2, starting transfers between devices, shifted(): return lax.ppermute(block, axis, route)  8.26 us
  transfers between devices with their start and end apart: 4, of which 4 were waited for; matrix products, arithmetic and copies ran while one was open for 0% of the time, Pallas kernels for 0%

commit v1 on v0

v1 whole, which is shorter than its diff:
```python
import jax
import jax.numpy as jnp
import numpy as np
from jax import lax
from jax.experimental import pallas as pl
from jax.experimental.pallas import tpu as pltpu
from jax.sharding import PartitionSpec as P

MESH = pl.DeviceIdType.MESH
ROWS = 64
COLS = 128
F32 = jnp.float32
BF16 = jnp.bfloat16


def shifted(block, axis, distance):
    devices = range(lax.axis_size(axis))
    route = [(i - distance, i) for i in devices if i - distance in devices]
    return lax.ppermute(block, axis, route)


def local_conv(block, weight, pad_rows, row_count, col_count):
    channels = block.shape[0]
    slices = block.shape[1]
    volume = block.reshape(1, channels, slices, row_count, col_count)
    kernel = weight.reshape(3, 3, 3, weight.shape[1], weight.shape[2])
    return lax.conv_general_dilated(
        volume,
        kernel,
        (2, 2, 2),
        ((0, 0), (pad_rows, pad_rows), (1, 1)),
        dimension_numbers=("NCDHW", "DHWOI", "NCDHW"),
        preferred_element_type=F32,
    )[0]


def activate(summed, bias_vec):
    summed = summed + bias_vec.astype(F32)[:, None, None, None]
    return jnp.where(summed > 0, summed, 0.2 * summed).astype(BF16)


def gathered(volume_in, filters_a, bias_a, filters_b, bias_b):
    slices = volume_in.shape[1]
    outputs = filters_a.shape[1]
    extended = jnp.concatenate([shifted(volume_in[:, -1:], "spatial", 1), volume_in], 1)
    full = lax.all_gather(extended, "filter", axis=0, tiled=True)
    hidden = activate(local_conv(full, filters_a, 1, ROWS, COLS), bias_a)
    hidden = hidden.reshape(outputs, slices // 2, ROWS // 2 * (COLS // 2))
    extended = jnp.concatenate([shifted(hidden[:, -1:], "spatial", 1), hidden], 1)
    full = lax.all_gather(extended, "filter", axis=0, tiled=True)
    out = activate(local_conv(full, filters_b, 1, ROWS // 2, COLS // 2), bias_b)
    return out.reshape(filters_b.shape[1], slices // 4, ROWS // 4 * (COLS // 4))


HALF = 2048
QUARTER = 512


def pick_first():
    s = np.zeros((256, 3, 128), np.float32)
    for l in range(3):
        for row in range(2):
            for w in range(64):
                source = 2 * w + l - 1
                if source >= 0:
                    s[row * 128 + source, l, row * 64 + w] = 1
    return s.reshape(256, 384)


def pick_second():
    s = np.zeros((2, 512, 3, 128), np.float32)
    for half in range(2):
        for l in range(3):
            for row in range(4):
                for w in range(32):
                    source = 2 * w + l - 1
                    if source >= 0:
                        s[half, row * 128 + half * 64 + source, l, row * 32 + w] = 1
    return s.reshape(2, 512, 384)


def leaky(u):
    return jnp.where(u > 0, u, 0.2 * u).astype(BF16)


def kernel(
    n_spatial, x, fa, fb, ba, bb, s1, s2, out,
    xh, wa_send, wa, wb_send, wb, v0, v1, part, sib, y_send, y_recv, hid, v2,
    part2, sib2, z_send, z_recv,
    halo_sems, wa_sems, wb_sems, sib_sems, y_sems, hid_sems, sib2_sems, z_sems,
):
    s = lax.axis_index("spatial")
    f = lax.axis_index("filter")
    core, chip = f % 2, f // 2
    sibling = chip * 2 + (1 - core)
    partner = (1 - chip) * 2 + core
    diagonal = (1 - chip) * 2 + (1 - core)
    slot = core * 2 + chip
    peers = (diagonal, partner, sibling)
    is_first, is_last = s == 0, s == n_spatial - 1

    barrier = pltpu.get_barrier_semaphore()
    for peer in peers:
        pl.semaphore_signal(barrier, inc=1, device_id=(s, peer), device_id_type=MESH)

    @pl.when(jnp.logical_not(is_last))
    def _():
        pl.semaphore_signal(barrier, inc=1, device_id=(s + 1, f), device_id_type=MESH)

    @pl.when(jnp.logical_not(is_first))
    def _():
        pl.semaphore_signal(barrier, inc=1, device_id=(s - 1, f), device_id_type=MESH)

    for g in range(4):
        to = (g % 2) * 2 + g // 2
        for b in range(7):
            parts = [fa[t][:, 32 * g : 32 * g + 32] for t in range(4 * b, min(4 * b + 4, 27))]
            if len(parts) < 4:
                parts.append(jnp.zeros((64, 32), BF16))
            wa_send[to, :, 128 * b : 128 * b + 128] = jnp.concatenate(parts, axis=1)

    at_end = jnp.logical_or(is_first, is_last)

    @pl.when(at_end)
    def _():
        pl.semaphore_wait(barrier, 4)

    @pl.when(jnp.logical_not(at_end))
    def _():
        pl.semaphore_wait(barrier, 5)

    def remote(src, dst, sems, target):
        return pltpu.make_async_remote_copy(
            src_ref=src, dst_ref=dst, send_sem=sems[0], recv_sem=sems[1],
            device_id=target, device_id_type=MESH,
        )

    def pair(sems, *index):
        return sems.at[(0,) + index], sems.at[(1,) + index]

    def slot_of(peer):
        return (peer % 2) * 2 + peer // 2

    def weight_copy(send, dst, sems, m):
        return remote(send.at[slot_of(peers[m])], dst.at[slot], pair(sems, m), (s, peers[m]))

    for m in range(3):
        weight_copy(wa_send, wa, wa_sems, m).start()
    halo = remote(x.at[pl.ds(96, 32)], xh, pair(halo_sems), (s + 1, f))

    @pl.when(jnp.logical_not(is_last))
    def _():
        halo.start()

    wa[slot] = wa_send[slot]

    for g in range(4):
        to = (g % 2) * 2 + g // 2
        for b in range(14):
            parts = [fb[t][:, 64 * g : 64 * g + 64] for t in range(2 * b, min(2 * b + 2, 27))]
            if len(parts) < 2:
                parts.append(jnp.zeros((64, 64), BF16))
            wb_send[to, :, 128 * b : 128 * b + 128] = jnp.concatenate(parts, axis=1)
    for m in range(3):
        weight_copy(wb_send, wb, wb_sems, m).start()
    wb[slot] = wb_send[slot]

    def rows_of(ref, t):
        def row(r):
            return ref[:, pl.ds(pl.multiple_of(r * 128, 128), 128)]

        before = jnp.where(t > 0, row(jnp.maximum(4 * t - 1, 0)), jnp.zeros((), BF16))
        one = row(4 * t + 1)
        return (
            jnp.concatenate([before, one], 1),
            jnp.concatenate([row(4 * t), row(4 * t + 2)], 1),
            jnp.concatenate([one, row(4 * t + 3)], 1),
        )

    def taps_own(t, carry):
        cells = jnp.concatenate(rows_of(x, t), 0)
        picked = jnp.dot(cells, s1[...], preferred_element_type=F32).astype(BF16)
        lanes = pl.ds(pl.multiple_of(t * 128, 128), 128)
        for j in range(3):
            for l in range(3):
                for k in range(4):
                    piece = picked[j * 128 + k * 32 : j * 128 + k * 32 + 32, l * 128 : l * 128 + 128]
                    if k > 0:
                        at = ((k - 1) * 9 + 3 * j + l) * 32
                        v1[at : at + 32, lanes] = piece
                    if k < 2:
                        at = ((k + 1) * 9 + 3 * j + l) * 32
                        v0[at : at + 32, lanes] = piece
        return carry

    v0[864:896] = jnp.zeros((32, HALF), BF16)
    v1[864:896] = jnp.zeros((32, HALF), BF16)
    lax.fori_loop(0, 16, taps_own, 0)

    def taps_halo(q, carry):
        cells = jnp.concatenate([c for t in range(4) for c in rows_of(xh, 4 * q + t)], 0)
        picked = jnp.dot(cells, s1[...], preferred_element_type=F32).astype(BF16)
        for t in range(4):
            lanes = pl.ds(pl.multiple_of((4 * q + t) * 128, 128), 128)
            for j in range(3):
                for l in range(3):
                    at = (3 * j + l) * 32
                    row = (3 * t + j) * 32
                    v0[at : at + 32, lanes] = picked[row : row + 32, l * 128 : l * 128 + 128]
        return carry

    def sib_copy(h, u):
        return remote(part.at[h, u, 1 - core], sib.at[h, u], pair(sib_sems, h, u), (s, sibling))

    def y_copy(h, u):
        return remote(y_send.at[h, u], y_recv.at[h, u], pair(y_sems, h, u), (s, partner))

    def first_conv(h, v):
        def body(u, carry):
            lanes = pl.ds(pl.multiple_of(u * 256, 256), 256)
            sums = jnp.dot(wa[...].reshape(256, 896), v[:, lanes], preferred_element_type=F32)
            part[h, u] = sums.reshape(2, 2, 64, 256)
            sib_copy(h, u).start()
            return carry

        lax.fori_loop(0, 8, body, 0)

    def across(h):
        def body(u, carry):
            sib_copy(h, u).wait_recv()
            y_send[h, u] = (part[h, u, core, 1 - chip] + sib[h, u, 1 - chip]).astype(BF16)
            y_copy(h, u).start()
            return carry

        lax.fori_loop(0, 8, body, 0)

    def finish(h, slot_h):
        bias = jnp.broadcast_to(ba[...], (64, 256))

        def body(u, carry):
            y_copy(h, u).wait_recv()
            total = part[h, u, core, chip] + sib[h, u, chip] + y_recv[h, u].astype(F32) + bias
            hid[slot_h, :, pl.ds(pl.multiple_of(u * 256, 256), 256)] = leaky(total)
            return carry

        lax.fori_loop(0, 8, body, 0)

    def second_taps(i):
        def block(q):
            return hid[i, :, 128 * q : 128 * q + 128]

        zero = jnp.zeros((64, 128), BF16)
        now = jnp.concatenate(
            [jnp.concatenate([block(4 * u + r) for r in range(4)], 1) for u in range(4)], 0
        )
        before = jnp.concatenate(
            [
                jnp.concatenate([block(4 * u + r - 1) if 4 * u + r else zero for r in range(4)], 1)
                for u in range(4)
            ],
            0,
        )
        for j, (cells, half) in enumerate(((before, 1), (now, 0), (now, 1))):
            picked = jnp.dot(cells, s2[half], preferred_element_type=F32).astype(BF16)
            for u in range(4):
                for l in range(3):
                    at = (i * 9 + 3 * j + l) * 64
                    v2[at : at + 64, 128 * u : 128 * u + 128] = picked[
                        64 * u : 64 * u + 64, 128 * l : 128 * l + 128
                    ]

    for m in range(3):
        weight_copy(wa_send, wa, wa_sems, m).wait_recv()
    first_conv(1, v1)

    @pl.when(is_first)
    def _():
        xh[...] = jnp.zeros(xh.shape, BF16)

    @pl.when(jnp.logical_not(is_first))
    def _():
        halo.wait_recv()

    across(1)
    lax.fori_loop(0, 4, taps_halo, 0)
    first_conv(0, v0)
    across(0)
    finish(1, 2)
    hid_halo = remote(hid.at[2], hid.at[0], pair(hid_sems), (s + 1, f))

    @pl.when(jnp.logical_not(is_last))
    def _():
        hid_halo.start()

    v2[1728:1792] = jnp.zeros((64, QUARTER), BF16)
    second_taps(2)
    finish(0, 1)
    second_taps(1)

    @pl.when(is_first)
    def _():
        hid[0] = jnp.zeros((64, HALF), BF16)

    @pl.when(jnp.logical_not(is_first))
    def _():
        hid_halo.wait_recv()

    second_taps(0)
    for m in range(3):
        weight_copy(wb_send, wb, wb_sems, m).wait_recv()

    def sib2_copy(u):
        return remote(part2.at[u, 1 - core], sib2.at[u], pair(sib2_sems, u), (s, sibling))

    def z_copy(u):
        return remote(z_send.at[u], z_recv.at[u], pair(z_sems, u), (s, partner))

    for u in range(2):
        lanes = slice(256 * u, 256 * u + 256)
        sums = jnp.dot(wb[...].reshape(256, 1792), v2[:, lanes], preferred_element_type=F32)
        part2[u] = sums.reshape(2, 2, 64, 256)
        sib2_copy(u).start()
    for u in range(2):
        sib2_copy(u).wait_recv()
        z_send[u] = (part2[u, core, 1 - chip] + sib2[u, 1 - chip]).astype(BF16)
        z_copy(u).start()
    bias = jnp.broadcast_to(bb[...], (64, 256))
    for u in range(2):
        z_copy(u).wait_recv()
        total = part2[u, core, chip] + sib2[u, chip] + z_recv[u].astype(F32) + bias
        out[:, 256 * u : 256 * u + 256] = leaky(total)

    for m in range(3):
        weight_copy(wa_send, wa, wa_sems, m).wait_send()
        weight_copy(wb_send, wb, wb_sems, m).wait_send()

    @pl.when(jnp.logical_not(is_last))
    def _():
        halo.wait_send()
        hid_halo.wait_send()

    for h in range(2):

        def drain(u, carry, h=h):
            sib_copy(h, u).wait_send()
            y_copy(h, u).wait_send()
            return carry

        lax.fori_loop(0, 8, drain, 0)
    for u in range(2):
        sib2_copy(u).wait_send()
        z_copy(u).wait_send()


def scattered(n_spatial, volume_in, filters_a, bias_a, filters_b, bias_b):
    x = jnp.transpose(volume_in, (1, 0, 2)).reshape(128, ROWS * COLS)
    vmem = pl.BlockSpec(memory_space=pltpu.VMEM)
    dma = pltpu.SemaphoreType.DMA

    def body(*refs):
        kernel(n_spatial, *refs)

    out = pl.pallas_call(
        body,
        out_shape=jax.ShapeDtypeStruct((64, QUARTER), BF16),
        in_specs=[vmem] * 7,
        out_specs=vmem,
        scratch_shapes=[
            pltpu.VMEM((32, ROWS * COLS), BF16),
            pltpu.VMEM((4, 64, 896), BF16),
            pltpu.VMEM((4, 64, 896), BF16),
            pltpu.VMEM((4, 64, 1792), BF16),
            pltpu.VMEM((4, 64, 1792), BF16),
            pltpu.VMEM((896, HALF), BF16),
            pltpu.VMEM((896, HALF), BF16),
            pltpu.VMEM((2, 8, 2, 2, 64, 256), F32),
            pltpu.VMEM((2, 8, 2, 64, 256), F32),
            pltpu.VMEM((2, 8, 64, 256), BF16),
            pltpu.VMEM((2, 8, 64, 256), BF16),
            pltpu.VMEM((3, 64, HALF), BF16),
            pltpu.VMEM((1792, QUARTER), BF16),
            pltpu.VMEM((2, 2, 2, 64, 256), F32),
            pltpu.VMEM((2, 2, 64, 256), F32),
            pltpu.VMEM((2, 64, 256), BF16),
            pltpu.VMEM((2, 64, 256), BF16),
            dma((2,)), dma((2, 3)), dma((2, 3)), dma((2, 2, 8)), dma((2, 2, 8)), dma((2,)),
            dma((2, 2)), dma((2, 2)),
        ],
        compiler_params=pltpu.CompilerParams(
            collective_id=0, has_side_effects=True, vmem_limit_bytes=52 * 1024 * 1024
        ),
        name="scattered_convs",
    )(
        x,
        filters_a,
        filters_b,
        bias_a.astype(F32).reshape(64, 1),
        bias_b.astype(F32).reshape(64, 1),
        jnp.asarray(pick_first(), BF16),
        jnp.asarray(pick_second(), BF16),
    )
    return out.reshape(64, 1, QUARTER)


def per_device(volume_in, filters_a, bias_a, filters_b, bias_b):
    if volume_in.shape == (32, 4, ROWS * COLS) and filters_b.shape == (27, 64, 256):
        return scattered(lax.axis_size("spatial"), volume_in, filters_a, bias_a, filters_b, bias_b)
    return gathered(volume_in, filters_a, bias_a, filters_b, bias_b)


def solution(mesh):
    in_specs = (
        P("filter", "spatial", None),
        P(None, "filter", None),
        P("filter"),
        P(None, "filter", None),
        P("filter"),
    )
    return jax.shard_map(
        per_device,
        mesh=mesh,
        in_specs=in_specs,
        out_specs=P("filter", "spatial", None),
        check_vma=False,
    )
```

time: 225 us -> 46.6 us (0.21)
  waiting for transfers between devices: 119 us -> 0 us
  local copies, waits for them, and re-layouts: 66.2 us -> 5.03 us
  Pallas kernels: 0 us -> 40 us
  between operations: 13.6 us -> 0.03 us
  matrix products: 12.7 us -> 0 us
  starting transfers between devices: 8.31 us -> 0 us
  other arithmetic: 3.7 us -> 1.31 us
    all_gather x2 -> x0, waiting for transfers between devices: 102 us -> none  [the longest x1 72.5 us: per_device(): lax.all_gather(extended, 'filter', axis=0, tiled=True)]
    pallas_call x0 -> x1, Pallas kernels: none -> 40 us  [scattered(): pl.pallas_call(body, out_shape=jax.ShapeDtypeStruct((64, QUARTER), BF16),...]
    unnamed x15 -> x7, local copies, waits for them, and re-layouts: 21.3 us -> 0.65 us
    all_gather x2 -> x0, local copies, waits for them, and re-layouts: 18.8 us -> none  [the longest x1 14.2 us: per_device(): lax.all_gather(extended, 'filter', axis=0, tiled=True)]
    ppermute x2 -> x0, waiting for transfers between devices: 17.1 us -> none  [shifted(): return lax.ppermute(block, axis, route)]
    conv_general_dilated x10 -> x0, local copies, waits for them, and re-layouts: 17 us -> none  [local_conv(): lax.conv_general_dilated(volume, kernel, (2, 2, 2), ((0, 0), (pad_rows, p...]
    conv_general_dilated x2 -> x0, matrix products: 12.7 us -> none  [local_conv(): lax.conv_general_dilated(volume, kernel, (2, 2, 2), ((0, 0), (pad_rows, p...]
    ppermute x2 -> x0, starting transfers between devices: 8.26 us -> none  [shifted(): return lax.ppermute(block, axis, route)]
  transfers between devices with their start and end apart: 4 -> 0, of which waited for: 4 -> 0; matrix products, arithmetic and copies ran while one was open for 0% -> 0% of each run, Pallas kernels for 0% -> 0%
where the time goes in v1:
time: 46.6 us; the launch traced here: 46.4 us
  Pallas kernels  40 us (86%)
  local copies, waits for them, and re-layouts  5.03 us (11%)
  other arithmetic  1.31 us (3%)
    pallas_call x1, Pallas kernels, scattered(): pl.pallas_call(body, out_shape=jax.ShapeDtypeStruct((64, QUARTER), BF16),...  40 us
    transpose x1, local copies, waits for them, and re-layouts, scattered(): x = jnp.transpose(volume_in, (1, 0, 2)).reshape(128, ROWS * COLS)  4.19 us

profile of v1, /device:TPU:0, one launch (start us, length us, event | category | flops | bytes accessed | tf_op | source)
XLA Modules:
  0.0 46.4 jit_solution(8347298005794208255)
XLA Ops:
  0.0 0.7 %bitcast_convert_fusion.1 = f32[64,1]{0,1:T(1,128)S(1)} fusion(bf16[64]{0:T(256)(128)(2,1)} %param.9), kind=kLoop, calls=%fused_computation.1 | loop fusion | flops 64 | bytes 384 | tf_op jit(solution)/shard_map/reshape | solution.py:397
  0.7 0.7 %bitcast_convert_fusion = f32[64,1]{0,1:T(1,128)S(1)} fusion(bf16[64]{0:T(256)(128)(2,1)} %param.11), kind=kLoop, calls=%fused_computation | loop fusion | flops 64 | bytes 384 | tf_op jit(solution)/shard_map/reshape | solution.py:398
  1.3 0.1 copy.10.refs_4_
  1.4 0.1 copy.9.refs_3_
  1.5 0.0 copy-start
  1.5 0.0 copy-start.1
  1.5 0.0 copy-start.2
  1.5 4.2 %copy.8 = bf16[4,32,8192]{2,1,0:T(8,128)(2,1)} copy(bf16[4,32,8192]{2,0,1:T(4,128)(2,1)} %bitcast.11) | data formatting | bytes 4194304 | tf_op jit(solution)/shard_map/transpose | solution.py:356
  5.7 0.0 copy-done
  5.7 0.0 copy-done.1
  5.7 0.0 copy-done.2
  5.7 40.0 %scattered_convs.1 = bf16[64,512]{1,0:T(8,128)(2,1)S(1)} custom-call(bf16[128,8192]{1,0:T(8,128)(2,1)} %bitcast.10, bf16[27,64,128]{2,1,0:T(8,128)(2,1)S(1)} %copy-done.1, bf16[27,64,256]{2,1,0:T(8,128)(2,1)} %refs_2_.1, f32[64,1]{1,0:T(8,128)S(1)} %copy.9.refs_3_, f32[64,1]{1,0:T(8,128)S(1)} %copy.10.refs_4_, bf16[256,384]{1,0:T(8,128)(2,1)S(1)} %copy-done.2, ...), custom_call_target="tpu_custom_call" | custom-call | tf_op jit(solution)/shard_map/scattered_convs/pallas_call | solution.py:363
  45.7 0.6 %copy.12 = bf16[64,1,512]{2,0,1:T(8,128)(2,1)} copy(bf16[64,1,512]{2,0,1:T(8,128)(2,1)S(1)} %bitcast.9) | data formatting | bytes 131072
Async XLA Ops:
  1.5 4.2 %copy-start = (bf16[2,512,384]{2,1,0:T(8,128)(2,1)S(1)}, bf16[2,512,384]{2,1,0:T(8,128)(2,1)}, u32[]{:S(2)}) copy-start(bf16[2,512,384]{2,1,0:T(8,128)(2,1)} %constant.5.clone.refs_6_) | copy-start | bytes 2359300
  1.5 4.2 %copy-start.1 = (bf16[27,64,128]{2,1,0:T(8,128)(2,1)S(1)}, bf16[27,64,128]{2,1,0:T(8,128)(2,1)}, u32[]{:S(2)}) copy-start(bf16[27,64,128]{2,1,0:T(8,128)(2,1)} %refs_1_.1) | copy-start | bytes 1327108
  1.5 4.2 %copy-start.2 = (bf16[256,384]{1,0:T(8,128)(2,1)S(1)}, bf16[256,384]{1,0:T(8,128)(2,1)}, u32[]{:S(2)}) copy-start(bf16[256,384]{1,0:T(8,128)(2,1)} %constant.4.clone.refs_5_) | copy-start | bytes 589828

commit v2 on v1

--- a/solution.py
+++ b/solution.py
@@ -84,10 +84,10 @@
 
 
 def kernel(
-    n_spatial, x, fa, fb, ba, bb, s1, s2, out,
-    xh, wa_send, wa, wb_send, wb, v0, v1, part, sib, y_send, y_recv, hid, v2,
+    n_spatial, xin, fa, fb_in, ba, bb, s1_in, s2_in, out,
+    fb, s1, s2, xv, x, xh, wa_send, wa, wb_send, wb, v0, v1, part, sib, y_send, y_recv, hid, v2,
     part2, sib2, z_send, z_recv,
-    halo_sems, wa_sems, wb_sems, sib_sems, y_sems, hid_sems, sib2_sems, z_sems,
+    in_sems, x_sem, halo_sems, wa_sems, wb_sems, sib_sems, y_sems, hid_sems, sib2_sems, z_sems,
 ):
     s = lax.axis_index("spatial")
     f = lax.axis_index("filter")
@@ -98,10 +98,21 @@
     slot = core * 2 + chip
     peers = (diagonal, partner, sibling)
     is_first, is_last = s == 0, s == n_spatial - 1
-
+    half = (s // 2) % 2
+    mate = s + 2 - 4 * half
+
+    load = pltpu.make_async_copy(xin, xv, x_sem)
+    load.start()
+    load_fb = pltpu.make_async_copy(fb_in, fb, in_sems.at[0])
+    load_s1 = pltpu.make_async_copy(s1_in, s1, in_sems.at[1])
+    load_s2 = pltpu.make_async_copy(s2_in, s2, in_sems.at[2])
+    load_fb.start()
+    load_s1.start()
+    load_s2.start()
     barrier = pltpu.get_barrier_semaphore()
     for peer in peers:
         pl.semaphore_signal(barrier, inc=1, device_id=(s, peer), device_id_type=MESH)
+    pl.semaphore_signal(barrier, inc=1, device_id=(mate, f), device_id_type=MESH)
 
     @pl.when(jnp.logical_not(is_last))
     def _():
@@ -117,17 +128,19 @@
             parts = [fa[t][:, 32 * g : 32 * g + 32] for t in range(4 * b, min(4 * b + 4, 27))]
             if len(parts) < 4:
                 parts.append(jnp.zeros((64, 32), BF16))
-            wa_send[to, :, 128 * b : 128 * b + 128] = jnp.concatenate(parts, axis=1)
+            block = jnp.concatenate(parts, axis=1)
+            for q in range(2):
+                wa_send[to, q, :, 128 * b : 128 * b + 128] = block[32 * q : 32 * q + 32]
 
     at_end = jnp.logical_or(is_first, is_last)
 
     @pl.when(at_end)
     def _():
-        pl.semaphore_wait(barrier, 4)
+        pl.semaphore_wait(barrier, 5)
 
     @pl.when(jnp.logical_not(at_end))
     def _():
-        pl.semaphore_wait(barrier, 5)
+        pl.semaphore_wait(barrier, 6)
 
     def remote(src, dst, sems, target):
         return pltpu.make_async_remote_copy(
@@ -142,28 +155,66 @@
         return (peer % 2) * 2 + peer // 2
 
     def weight_copy(send, dst, sems, m):
-        return remote(send.at[slot_of(peers[m])], dst.at[slot], pair(sems, m), (s, peers[m]))
+        if m == 2 or send is wa_send or send is wb_send:
+            return remote(send.at[slot_of(peers[m])], dst.at[slot], pair(sems, m), (s, peers[m]))
+        return remote(
+            send.at[slot_of(peers[m]), half], dst.at[slot, half], pair(sems, m), (s, peers[m])
+        )
+
+    def forward_copy(dst, sems, m):
+        block = dst.at[slot_of(peers[m]), half]
+        return remote(block, block, pair(sems, 3 + m), (mate, f))
+
+    def forward(send, dst, sems):
+        if send is wa_send or send is wb_send:
+            return
+        for m in range(2):
+            weight_copy(send, dst, sems, m).wait_recv()
+            forward_copy(dst, sems, m).start()
+
+    def weights_here(send, dst, sems):
+        weight_copy(send, dst, sems, 2).wait_recv()
+        for m in range(2):
+            if send is wa_send or send is wb_send:
+                weight_copy(send, dst, sems, m).wait_recv()
+                continue
+            forward_copy(dst, sems, m).wait_recv()
 
     for m in range(3):
         weight_copy(wa_send, wa, wa_sems, m).start()
-    halo = remote(x.at[pl.ds(96, 32)], xh, pair(halo_sems), (s + 1, f))
-
-    @pl.when(jnp.logical_not(is_last))
-    def _():
-        halo.start()
-
     wa[slot] = wa_send[slot]
 
+    load_fb.wait()
     for g in range(4):
         to = (g % 2) * 2 + g // 2
         for b in range(14):
             parts = [fb[t][:, 64 * g : 64 * g + 64] for t in range(2 * b, min(2 * b + 2, 27))]
             if len(parts) < 2:
                 parts.append(jnp.zeros((64, 64), BF16))
-            wb_send[to, :, 128 * b : 128 * b + 128] = jnp.concatenate(parts, axis=1)
+            block = jnp.concatenate(parts, axis=1)
+            for q in range(2):
+                wb_send[to, q, :, 128 * b : 128 * b + 128] = block[32 * q : 32 * q + 32]
     for m in range(3):
         weight_copy(wb_send, wb, wb_sems, m).start()
     wb[slot] = wb_send[slot]
+
+    load.wait()
+    load_s1.wait()
+
+    def by_slice(q, carry):
+        lanes = pl.ds(pl.multiple_of(q * 512, 512), 512)
+        rows = jnp.swapaxes(xv[:, :, lanes], 0, 1)
+        for k in range(4):
+            x[32 * k : 32 * k + 32, lanes] = rows[k]
+        return carry
+
+    lax.fori_loop(0, 16, by_slice, 0)
+    halo = remote(x.at[pl.ds(96, 32)], xh, pair(halo_sems), (s + 1, f))
+
+    @pl.when(jnp.logical_not(is_last))
+    def _():
+        halo.start()
+
 
     def rows_of(ref, t):
         def row(r):
@@ -195,7 +246,9 @@
 
     v0[864:896] = jnp.zeros((32, HALF), BF16)
     v1[864:896] = jnp.zeros((32, HALF), BF16)
-    lax.fori_loop(0, 16, taps_own, 0)
+    lax.fori_loop(0, 10, taps_own, 0)
+    forward(wa_send, wa, wa_sems)
+    lax.fori_loop(10, 16, taps_own, 0)
 
     def taps_halo(q, carry):
         cells = jnp.concatenate([c for t in range(4) for c in rows_of(xh, 4 * q + t)], 0)
@@ -215,39 +268,54 @@
     def y_copy(h, u):
         return remote(y_send.at[h, u], y_recv.at[h, u], pair(y_sems, h, u), (s, partner))
 
+    def across_one(h, u):
+        sib_copy(h, u).wait_recv()
+        y_send[h, u] = (part[h, u, core, 1 - chip] + sib[h, u, 1 - chip]).astype(BF16)
+        y_copy(h, u).start()
+
+    def across(h):
+        across_one(h, 5)
+        across_one(h, 6)
+        across_one(h, 7)
+
     def first_conv(h, v):
         def body(u, carry):
             lanes = pl.ds(pl.multiple_of(u * 256, 256), 256)
             sums = jnp.dot(wa[...].reshape(256, 896), v[:, lanes], preferred_element_type=F32)
             part[h, u] = sums.reshape(2, 2, 64, 256)
             sib_copy(h, u).start()
+
+            @pl.when(u >= 3)
+            def _():
+                across_one(h, u - 3)
+
             return carry
 
         lax.fori_loop(0, 8, body, 0)
 
-    def across(h):
-        def body(u, carry):
-            sib_copy(h, u).wait_recv()
-            y_send[h, u] = (part[h, u, core, 1 - chip] + sib[h, u, 1 - chip]).astype(BF16)
-            y_copy(h, u).start()
-            return carry
-
-        lax.fori_loop(0, 8, body, 0)
+    def hid_copy(u):
+        return remote(hid.at[2, u], hid.at[0, u], pair(hid_sems, u), (s + 1, f))
 
     def finish(h, slot_h):
-        bias = jnp.broadcast_to(ba[...], (64, 256))
+        bias = jnp.broadcast_to(ba[...].astype(F32), (64, 256))
 
         def body(u, carry):
             y_copy(h, u).wait_recv()
             total = part[h, u, core, chip] + sib[h, u, chip] + y_recv[h, u].astype(F32) + bias
-            hid[slot_h, :, pl.ds(pl.multiple_of(u * 256, 256), 256)] = leaky(total)
+            hid[slot_h, u] = leaky(total)
+            if slot_h == 2:
+
+                @pl.when(jnp.logical_not(is_last))
+                def _():
+                    hid_copy(u).start()
+
             return carry
 
         lax.fori_loop(0, 8, body, 0)
 
     def second_taps(i):
         def block(q):
-            return hid[i, :, 128 * q : 128 * q + 128]
+            return hid[i, q // 2, :, 128 * (q % 2) : 128 * (q % 2) + 128]
 
         zero = jnp.zeros((64, 128), BF16)
         now = jnp.concatenate(
@@ -269,9 +337,9 @@
                         64 * u : 64 * u + 64, 128 * l : 128 * l + 128
                     ]
 
-    for m in range(3):
-        weight_copy(wa_send, wa, wa_sems, m).wait_recv()
+    weights_here(wa_send, wa, wa_sems)
     first_conv(1, v1)
+    forward(wb_send, wb, wb_sems)
 
     @pl.when(is_first)
     def _():
@@ -286,58 +354,61 @@
     first_conv(0, v0)
     across(0)
     finish(1, 2)
-    hid_halo = remote(hid.at[2], hid.at[0], pair(hid_sems), (s + 1, f))
-
-    @pl.when(jnp.logical_not(is_last))
-    def _():
-        hid_halo.start()
-
     v2[1728:1792] = jnp.zeros((64, QUARTER), BF16)
+    load_s2.wait()
     second_taps(2)
     finish(0, 1)
     second_taps(1)
 
     @pl.when(is_first)
     def _():
-        hid[0] = jnp.zeros((64, HALF), BF16)
+        hid[0] = jnp.zeros((8, 64, 256), BF16)
 
     @pl.when(jnp.logical_not(is_first))
     def _():
-        hid_halo.wait_recv()
+        for u in range(8):
+            hid_copy(u).wait_recv()
 
     second_taps(0)
-    for m in range(3):
-        weight_copy(wb_send, wb, wb_sems, m).wait_recv()
+    weights_here(wb_send, wb, wb_sems)
 
     def sib2_copy(u):
-        return remote(part2.at[u, 1 - core], sib2.at[u], pair(sib2_sems, u), (s, sibling))
-
-    def z_copy(u):
-        return remote(z_send.at[u], z_recv.at[u], pair(z_sems, u), (s, partner))
+        block = part2.at[u, 1 - core, chip]
+        return remote(block, sib2.at[u], pair(sib2_sems, u), (s, sibling))
+
+    def z_copy(u, m):
+        return remote(z_send.at[u, m], z_recv.at[u, m], pair(z_sems, u, m), (s, peers[m]))
 
     for u in range(2):
         lanes = slice(256 * u, 256 * u + 256)
         sums = jnp.dot(wb[...].reshape(256, 1792), v2[:, lanes], preferred_element_type=F32)
         part2[u] = sums.reshape(2, 2, 64, 256)
+        for m in range(2):
+            to_core = 1 - core if m == 0 else core
+            z_send[u, m] = part2[u, to_core, 1 - chip].astype(BF16)
+            z_copy(u, m).start()
         sib2_copy(u).start()
+    bias = jnp.broadcast_to(bb[...].astype(F32), (64, 256))
     for u in range(2):
         sib2_copy(u).wait_recv()
-        z_send[u] = (part2[u, core, 1 - chip] + sib2[u, 1 - chip]).astype(BF16)
-        z_copy(u).start()
-    bias = jnp.broadcast_to(bb[...], (64, 256))
-    for u in range(2):
-        z_copy(u).wait_recv()
-        total = part2[u, core, chip] + sib2[u, chip] + z_recv[u].astype(F32) + bias
+        for m in range(2):
+            z_copy(u, m).wait_recv()
+        far = z_recv[u, 0].astype(F32) + z_recv[u, 1].astype(F32)
+        total = part2[u, core, chip] + sib2[u] + far + bias
         out[:, 256 * u : 256 * u + 256] = leaky(total)
 
     for m in range(3):
         weight_copy(wa_send, wa, wa_sems, m).wait_send()
         weight_copy(wb_send, wb, wb_sems, m).wait_send()
+    for m in range(2):
+        pass
+        pass
 
     @pl.when(jnp.logical_not(is_last))
     def _():
         halo.wait_send()
-        hid_halo.wait_send()
+        for u in range(8):
+            hid_copy(u).wait_send()
 
     for h in range(2):
 
@@ -349,12 +420,13 @@
         lax.fori_loop(0, 8, drain, 0)
     for u in range(2):
         sib2_copy(u).wait_send()
-        z_copy(u).wait_send()
+        for m in range(2):
+            z_copy(u, m).wait_send()
 
 
 def scattered(n_spatial, volume_in, filters_a, bias_a, filters_b, bias_b):
-    x = jnp.transpose(volume_in, (1, 0, 2)).reshape(128, ROWS * COLS)
     vmem = pl.BlockSpec(memory_space=pltpu.VMEM)
+    hbm = pl.BlockSpec(memory_space=pl.ANY)
     dma = pltpu.SemaphoreType.DMA
 
     def body(*refs):
@@ -363,39 +435,44 @@
     out = pl.pallas_call(
         body,
         out_shape=jax.ShapeDtypeStruct((64, QUARTER), BF16),
-        in_specs=[vmem] * 7,
+        in_specs=[hbm, vmem, hbm, vmem, vmem, hbm, hbm],
         out_specs=vmem,
         scratch_shapes=[
+            pltpu.VMEM((27, 64, 256), BF16),
+            pltpu.VMEM((256, 384), BF16),
+            pltpu.VMEM((2, 512, 384), BF16),
+            pltpu.VMEM((32, 4, ROWS * COLS), BF16),
+            pltpu.VMEM((128, ROWS * COLS), BF16),
             pltpu.VMEM((32, ROWS * COLS), BF16),
-            pltpu.VMEM((4, 64, 896), BF16),
-            pltpu.VMEM((4, 64, 896), BF16),
-            pltpu.VMEM((4, 64, 1792), BF16),
-            pltpu.VMEM((4, 64, 1792), BF16),
+            pltpu.VMEM((4, 2, 32, 896), BF16),
+            pltpu.VMEM((4, 2, 32, 896), BF16),
+            pltpu.VMEM((4, 2, 32, 1792), BF16),
+            pltpu.VMEM((4, 2, 32, 1792), BF16),
             pltpu.VMEM((896, HALF), BF16),
             pltpu.VMEM((896, HALF), BF16),
             pltpu.VMEM((2, 8, 2, 2, 64, 256), F32),
             pltpu.VMEM((2, 8, 2, 64, 256), F32),
             pltpu.VMEM((2, 8, 64, 256), BF16),
             pltpu.VMEM((2, 8, 64, 256), BF16),
-            pltpu.VMEM((3, 64, HALF), BF16),
+            pltpu.VMEM((3, 8, 64, 256), BF16),
             pltpu.VMEM((1792, QUARTER), BF16),
             pltpu.VMEM((2, 2, 2, 64, 256), F32),
-            pltpu.VMEM((2, 2, 64, 256), F32),
-            pltpu.VMEM((2, 64, 256), BF16),
-            pltpu.VMEM((2, 64, 256), BF16),
-            dma((2,)), dma((2, 3)), dma((2, 3)), dma((2, 2, 8)), dma((2, 2, 8)), dma((2,)),
-            dma((2, 2)), dma((2, 2)),
+            pltpu.VMEM((2, 64, 256), F32),
+            pltpu.VMEM((2, 2, 64, 256), BF16),
+            pltpu.VMEM((2, 2, 64, 256), BF16),
+            dma((3,)), dma, dma((2,)), dma((2, 5)), dma((2, 5)), dma((2, 2, 8)), dma((2, 2, 8)), dma((2, 8)),
+            dma((2, 2)), dma((2, 2, 2)),
         ],
         compiler_params=pltpu.CompilerParams(
             collective_id=0, has_side_effects=True, vmem_limit_bytes=52 * 1024 * 1024
         ),
         name="scattered_convs",
     )(
-        x,
+        volume_in,
         filters_a,
         filters_b,
-        bias_a.astype(F32).reshape(64, 1),
-        bias_b.astype(F32).reshape(64, 1),
+        bias_a.reshape(64, 1),
+        bias_b.reshape(64, 1),
         jnp.asarray(pick_first(), BF16),
         jnp.asarray(pick_second(), BF16),
     )
@@ -403,8 +480,10 @@
 
 
 def per_device(volume_in, filters_a, bias_a, filters_b, bias_b):
-    if volume_in.shape == (32, 4, ROWS * COLS) and filters_b.shape == (27, 64, 256):
-        return scattered(lax.axis_size("spatial"), volume_in, filters_a, bias_a, filters_b, bias_b)
+    n_spatial = lax.axis_size("spatial")
+    own = volume_in.shape == (32, 4, ROWS * COLS) and filters_b.shape == (27, 64, 256)
+    if own and n_spatial % 4 == 0:
+        return scattered(n_spatial, volume_in, filters_a, bias_a, filters_b, bias_b)
     return gathered(volume_in, filters_a, bias_a, filters_b, bias_b)
 
 

time: 46.6 us -> 43.9 us (0.942)
  Pallas kernels: 40 us -> 38.4 us
  other arithmetic: 1.31 us -> 0 us
    transpose x1 -> x0, local copies, waits for them, and re-layouts: 4.19 us -> none  [scattered(): x = jnp.transpose(volume_in, (1, 0, 2)).reshape(128, ROWS * COLS)]
    unnamed x7, local copies, waits for them, and re-layouts: 0.65 us -> 3.7 us
    pallas_call x1, Pallas kernels: 40 us -> 38.4 us  [scattered(): pl.pallas_call(body, out_shape=jax.ShapeDtypeStruct((64, QUARTER), BF16),...]
    reshape x2, local copies, waits for them, and re-layouts: 0.19 us -> 1.52 us  [the longest x1 0.76 us: scattered(): bias_b.reshape(64, 1)]
    reshape x2 -> x0, other arithmetic: 1.31 us -> none  [the longest x1 0.66 us: scattered(): bias_a.astype(F32).reshape(64, 1)]
where the time goes in v2:
time: 43.9 us; the launch traced here: 43.6 us
  Pallas kernels  38.4 us (87%)
  local copies, waits for them, and re-layouts  5.23 us (12%)
    pallas_call x1, Pallas kernels, scattered(): pl.pallas_call(body, out_shape=jax.ShapeDtypeStruct((64, QUARTER), BF16),...  38.4 us
    unnamed x7, local copies, waits for them, and re-layouts  3.7 us

profile of v2, /device:TPU:0, one launch (start us, length us, event | category | flops | bytes accessed | tf_op | source)
XLA Modules:
  0.0 43.6 jit_solution(13674906349822104596)
XLA Ops:
  0.0 0.8 %copy.8.refs_3_ = bf16[64,1]{1,0:T(8,128)(2,1)S(1)} copy(bf16[64,1]{0,1:T(2,128)(2,1)} %bitcast.4) | data formatting | bytes 256 | tf_op jit(solution)/shard_map/reshape | solution.py:474
  0.8 0.8 %copy.9.refs_4_ = bf16[64,1]{1,0:T(8,128)(2,1)S(1)} copy(bf16[64,1]{0,1:T(2,128)(2,1)} %bitcast.5) | data formatting | bytes 256 | tf_op jit(solution)/shard_map/reshape | solution.py:475
  1.5 0.0 copy-start
  1.5 1.1 %copy-done = bf16[2,512,384]{2,1,0:T(8,128)(2,1)S(1)} copy-done((bf16[2,512,384]{2,1,0:T(8,128)(2,1)S(1)}, bf16[2,512,384]{2,1,0:T(8,128)(2,1)}, u32[]{:S(2)}) %copy-start) | copy-done | bytes 786456
  2.7 0.0 copy-start.1
  2.7 1.0 %copy-done.1 = bf16[27,64,128]{2,1,0:T(8,128)(2,1)S(1)} copy-done((bf16[27,64,128]{2,1,0:T(8,128)(2,1)S(1)}, bf16[27,64,128]{2,1,0:T(8,128)(2,1)}, u32[]{:S(2)}) %copy-start.1) | copy-done | bytes 442392
  3.7 0.0 copy-start.2
  3.7 0.9 %copy-done.2 = bf16[256,384]{1,0:T(8,128)(2,1)S(1)} copy-done((bf16[256,384]{1,0:T(8,128)(2,1)S(1)}, bf16[256,384]{1,0:T(8,128)(2,1)}, u32[]{:S(2)}) %copy-start.2) | copy-done | bytes 196632
  4.6 38.4 %scattered_convs.1 = bf16[64,512]{1,0:T(8,128)(2,1)S(1)} custom-call(bf16[32,4,8192]{2,1,0:T(4,128)(2,1)} %refs_0_.1, bf16[27,64,128]{2,1,0:T(8,128)(2,1)S(1)} %copy-done.1, bf16[27,64,256]{2,1,0:T(8,128)(2,1)} %refs_2_.1, bf16[64,1]{1,0:T(8,128)(2,1)S(1)} %copy.8.refs_3_, bf16[64,1]{1,0:T(8,128)(2,1)S(1)} %copy.9.refs_4_, bf16[256,384]{1,0:T(8,128)(2,1)S(1)} %copy-done.2, ...), custom_call_target="tpu_custom_call" | custom-call | tf_op jit(solution)/shard_map/scattered_convs/pallas_call | solution.py:435
  43.0 0.6 %copy.11 = bf16[64,1,512]{2,0,1:T(8,128)(2,1)} copy(bf16[64,1,512]{2,0,1:T(8,128)(2,1)S(1)} %bitcast.3) | data formatting | bytes 131072
Async XLA Ops:
  1.5 1.1 %copy-start = (bf16[2,512,384]{2,1,0:T(8,128)(2,1)S(1)}, bf16[2,512,384]{2,1,0:T(8,128)(2,1)}, u32[]{:S(2)}) copy-start(bf16[2,512,384]{2,1,0:T(8,128)(2,1)} %constant.5.clone.refs_6_) | copy-start | bytes 2359300
  2.7 1.0 %copy-start.1 = (bf16[27,64,128]{2,1,0:T(8,128)(2,1)S(1)}, bf16[27,64,128]{2,1,0:T(8,128)(2,1)}, u32[]{:S(2)}) copy-start(bf16[27,64,128]{2,1,0:T(8,128)(2,1)} %refs_1_.1) | copy-start | bytes 1327108
  3.7 0.9 %copy-start.2 = (bf16[256,384]{1,0:T(8,128)(2,1)S(1)}, bf16[256,384]{1,0:T(8,128)(2,1)}, u32[]{:S(2)}) copy-start(bf16[256,384]{1,0:T(8,128)(2,1)} %constant.4.clone.refs_5_) | copy-start | bytes 589828

commit v3 on v2

--- a/solution.py
+++ b/solution.py
@@ -359,6 +359,11 @@
     second_taps(2)
     finish(0, 1)
     second_taps(1)
+    weights_here(wb_send, wb, wb_sems)
+    for u in range(2):
+        lanes = slice(256 * u, 256 * u + 256)
+        early = jnp.dot(wb[:, :, :, 640:].reshape(256, 1152), v2[640:, lanes], preferred_element_type=F32)
+        part2[u] = early.reshape(2, 2, 64, 256)
 
     @pl.when(is_first)
     def _():
@@ -370,7 +375,6 @@
             hid_copy(u).wait_recv()
 
     second_taps(0)
-    weights_here(wb_send, wb, wb_sems)
 
     def sib2_copy(u):
         block = part2.at[u, 1 - core, chip]
@@ -381,8 +385,8 @@
 
     for u in range(2):
         lanes = slice(256 * u, 256 * u + 256)
-        sums = jnp.dot(wb[...].reshape(256, 1792), v2[:, lanes], preferred_element_type=F32)
-        part2[u] = sums.reshape(2, 2, 64, 256)
+        late = jnp.dot(wb[:, :, :, :640].reshape(256, 640), v2[:640, lanes], preferred_element_type=F32)
+        part2[u] = part2[u] + late.reshape(2, 2, 64, 256)
         for m in range(2):
             to_core = 1 - core if m == 0 else core
             z_send[u, m] = part2[u, to_core, 1 - chip].astype(BF16)

time: 43.9 us -> 44 us (level)
  no operation moved by 1% of the time
where the time goes in v3:
time: 44 us; the launch traced here: 43.8 us
  Pallas kernels  38.5 us (88%)
  local copies, waits for them, and re-layouts  5.23 us (12%)
    pallas_call x1, Pallas kernels, scattered(): pl.pallas_call(body, out_shape=jax.ShapeDtypeStruct((64, QUARTER), BF16),...  38.5 us
    unnamed x7, local copies, waits for them, and re-layouts  3.7 us

profile of v3, /device:TPU:0, one launch (start us, length us, event | category | flops | bytes accessed | tf_op | source)
XLA Modules:
  0.0 43.8 jit_solution(16752604749352495313)
XLA Ops:
  0.0 0.8 %copy.8.refs_3_ = bf16[64,1]{1,0:T(8,128)(2,1)S(1)} copy(bf16[64,1]{0,1:T(2,128)(2,1)} %bitcast.4) | data formatting | bytes 256 | tf_op jit(solution)/shard_map/reshape | solution.py:478
  0.8 0.8 %copy.9.refs_4_ = bf16[64,1]{1,0:T(8,128)(2,1)S(1)} copy(bf16[64,1]{0,1:T(2,128)(2,1)} %bitcast.5) | data formatting | bytes 256 | tf_op jit(solution)/shard_map/reshape | solution.py:479
  1.5 0.0 copy-start
  1.5 1.1 %copy-done = bf16[2,512,384]{2,1,0:T(8,128)(2,1)S(1)} copy-done((bf16[2,512,384]{2,1,0:T(8,128)(2,1)S(1)}, bf16[2,512,384]{2,1,0:T(8,128)(2,1)}, u32[]{:S(2)}) %copy-start) | copy-done | bytes 786456
  2.7 0.0 copy-start.1
  2.7 1.0 %copy-done.1 = bf16[27,64,128]{2,1,0:T(8,128)(2,1)S(1)} copy-done((bf16[27,64,128]{2,1,0:T(8,128)(2,1)S(1)}, bf16[27,64,128]{2,1,0:T(8,128)(2,1)}, u32[]{:S(2)}) %copy-start.1) | copy-done | bytes 442392
  3.7 0.0 copy-start.2
  3.7 0.9 %copy-done.2 = bf16[256,384]{1,0:T(8,128)(2,1)S(1)} copy-done((bf16[256,384]{1,0:T(8,128)(2,1)S(1)}, bf16[256,384]{1,0:T(8,128)(2,1)}, u32[]{:S(2)}) %copy-start.2) | copy-done | bytes 196632
  4.6 38.5 %scattered_convs.1 = bf16[64,512]{1,0:T(8,128)(2,1)S(1)} custom-call(bf16[32,4,8192]{2,1,0:T(4,128)(2,1)} %refs_0_.1, bf16[27,64,128]{2,1,0:T(8,128)(2,1)S(1)} %copy-done.1, bf16[27,64,256]{2,1,0:T(8,128)(2,1)} %refs_2_.1, bf16[64,1]{1,0:T(8,128)(2,1)S(1)} %copy.8.refs_3_, bf16[64,1]{1,0:T(8,128)(2,1)S(1)} %copy.9.refs_4_, bf16[256,384]{1,0:T(8,128)(2,1)S(1)} %copy-done.2, ...), custom_call_target="tpu_custom_call" | custom-call | tf_op jit(solution)/shard_map/scattered_convs/pallas_call | solution.py:439
  43.1 0.6 %copy.11 = bf16[64,1,512]{2,0,1:T(8,128)(2,1)} copy(bf16[64,1,512]{2,0,1:T(8,128)(2,1)S(1)} %bitcast.3) | data formatting | bytes 131072
Async XLA Ops:
  1.5 1.1 %copy-start = (bf16[2,512,384]{2,1,0:T(8,128)(2,1)S(1)}, bf16[2,512,384]{2,1,0:T(8,128)(2,1)}, u32[]{:S(2)}) copy-start(bf16[2,512,384]{2,1,0:T(8,128)(2,1)} %constant.5.clone.refs_6_) | copy-start | bytes 2359300
  2.7 1.0 %copy-start.1 = (bf16[27,64,128]{2,1,0:T(8,128)(2,1)S(1)}, bf16[27,64,128]{2,1,0:T(8,128)(2,1)}, u32[]{:S(2)}) copy-start(bf16[27,64,128]{2,1,0:T(8,128)(2,1)} %refs_1_.1) | copy-start | bytes 1327108
  3.7 0.9 %copy-start.2 = (bf16[256,384]{1,0:T(8,128)(2,1)S(1)}, bf16[256,384]{1,0:T(8,128)(2,1)}, u32[]{:S(2)}) copy-start(bf16[256,384]{1,0:T(8,128)(2,1)} %constant.4.clone.refs_5_) | copy-start | bytes 589828
